TPU v7x, 256 devices: a whole 4x4x8 slice. The times are simulated.
256 devices in a mesh: rows: 32 (over y, z), cols: 8 (over x, core).
Axes of the slice: x: 4, y: 4, z: 8, core: 2. Of those that a mesh axis runs over, the one named last changes fastest.
Arguments:
- genotypes: int32 [20480, 4096], P('rows', 'cols'), may hold values from 0 to 2
- frequencies: float32 [4096], P('cols'), may hold values from 0.05 to 0.5
- traits: bfloat16 [20480, 32768], P('rows', 'cols'), may hold values from -6 to 6
- geno_sketch: bfloat16 [4096, 512], P('cols'), may hold values from -0.09375 to 0.09375
- trait_sketch: bfloat16 [32768, 512], P('cols'), may hold values from -0.03125 to 0.03125
- initial: float32 [512, 256], replicated, may hold values from -6 to 6
Outputs:
- geno_scores: bfloat16 [20480, 256], P('rows')
- trait_scores: bfloat16 [20480, 256], P('rows')
- geno_loadings: float32 [256, 4096], P('rows', 'cols')
- trait_loadings: float32 [256, 32768], P('rows', 'cols')
All inputs are finite; a program needn't handle non-finite values.
Results may differ from a plain program's by a relative error of at most 0.0059.
Values sent between devices are 32-bit elements; how exact they have to be, the bound alone decides.
A program may use at most 128 MiB of HBM per device.

v0:
```python
import math
import jax
import jax.numpy as jnp
from jax import lax
from jax.sharding import PartitionSpec as P


def standard(genotypes, frequencies):
    spread = lax.rsqrt(2.0 * frequencies * (1.0 - frequencies))
    return ((genotypes.astype(jnp.float32) - 2.0 * frequencies) * spread).astype(jnp.bfloat16)


def unit_columns(matrix):
    return matrix * lax.rsqrt(jnp.mean(matrix * matrix, axis=0, keepdims=True) + 1e-06)


def inner_product(left_side, right_side):
    return lax.dot_general(
        left_side,
        right_side,
        (((0,), (0,)), ((), ())),
        precision=lax.Precision.HIGHEST,
        preferred_element_type=jnp.float32,
    )


def on_device(genotypes, frequencies, traits, geno_sketch, trait_sketch, initial):
    people = genotypes.shape[0] * lax.axis_size("rows")
    sketch_width = geno_sketch.shape[1]
    standardized = standard(genotypes, frequencies)
    partial_geno = jnp.dot(standardized, geno_sketch, preferred_element_type=jnp.float32)
    partial_trait = jnp.dot(traits, trait_sketch, preferred_element_type=jnp.float32)
    sketch_geno, sketch_trait = lax.psum((partial_geno, partial_trait), "cols")
    gram_geno, gram_trait = lax.psum(
        (inner_product(sketch_geno, sketch_geno), inner_product(sketch_trait, sketch_trait)), "rows"
    )
    lower_geno = jnp.linalg.cholesky(gram_geno / people)
    lower_trait = jnp.linalg.cholesky(gram_trait / people)
    basis_geno = lax.linalg.triangular_solve(
        lower_geno, sketch_geno, left_side=False, lower=True, transpose_a=True
    )
    basis_trait = lax.linalg.triangular_solve(
        lower_trait, sketch_trait, left_side=False, lower=True, transpose_a=True
    )
    crossed = lax.psum(inner_product(basis_geno, basis_trait), "rows") / people
    left_dirs = unit_columns(jnp.dot(crossed, initial, precision=lax.Precision.HIGHEST))
    right_dirs = unit_columns(inner_product(crossed, left_dirs))
    root_sketch = math.sqrt(sketch_width)
    geno_scores = (
        jnp.dot(basis_geno, left_dirs, precision=lax.Precision.HIGHEST) / root_sketch
    ).astype(jnp.bfloat16)
    trait_scores = (
        jnp.dot(basis_trait, right_dirs, precision=lax.Precision.HIGHEST) / root_sketch
    ).astype(jnp.bfloat16)
    geno_width = standardized.shape[1]
    geno_term = lax.dot_general(
        geno_scores, standardized, (((0,), (0,)), ((), ())), preferred_element_type=jnp.float32
    )
    trait_term = lax.dot_general(
        trait_scores, traits, (((0,), (0,)), ((), ())), preferred_element_type=jnp.float32
    )
    summed = lax.psum_scatter(
        jnp.concatenate([geno_term, trait_term], axis=1), "rows", scatter_dimension=0, tiled=True
    )
    root_people = math.sqrt(people)
    geno_loadings = summed[:, :geno_width] / root_people
    trait_loadings = summed[:, geno_width:] / root_people
    return (geno_scores, trait_scores, geno_loadings, trait_loadings)


def solution(mesh):
    placed = (
        P("rows", "cols"),
        P("cols"),
        P("rows", "cols"),
        P("cols", None),
        P("cols", None),
        P(),
    )
    return jax.shard_map(
        on_device,
        mesh=mesh,
        in_specs=placed,
        out_specs=(P("rows", None), P("rows", None), P("rows", "cols"), P("rows", "cols")),
        check_vma=False,
    )
```

profile of v0, /device:TPU:2, one launch (start us, length us, event | category | flops | bytes accessed | tf_op | source)
XLA Modules:
  0.0 961.9 jit_solution(18372460097444687967)
XLA Ops:
  8.0 7.8 fusion.85
  17.4 73.2 %all-reduce.11.cloned.1.call-done = (f32[640,512]{1,0:T(8,128)}, f32[640,512]{1,0:T(8,128)}) async-done(((f32[640,512]{1,0:T(8,128)}, f32[640,512]{1,0:T(8,128)}), (f32[640,512]{1,0:T(8,128)}, f32[640,512]{1,0:T(8,128)})) %all-reduce.11.cloned.1.call-update) | async-done | bytes 2621456 | tf_op jit(solution)/shard_map/psum | solution.py:33
  90.6 5.5 fusion.84
  96.1 3.7 fusion.86
  100.0 156.1 %all-reduce.9.cloned.1.call-done = (f32[512,512]{0,1:T(8,128)}, f32[512,512]{0,1:T(8,128)}) async-done(((f32[512,512]{0,1:T(8,128)}, f32[512,512]{0,1:T(8,128)}), (f32[512,512]{0,1:T(8,128)}, f32[512,512]{0,1:T(8,128)})) %all-reduce.9.cloned.1.call-update) | async-done | bytes 2097168 | tf_op jit(solution)/shard_map/psum | solution.py:34
  261.5 2.7 fusion.2
  265.1 11.7 %cholesky.358 = f32[128,128]{1,0:T(8,128)S(1)} custom-call(f32[128,128]{1,0:T(8,128)S(1)} %cholesky.439), custom_call_target="Cholesky" | custom-call | tf_op jit(solution)/shard_map/jit(cholesky)/cholesky | solution.py:38
  276.9 11.7 %cholesky.286 = f32[128,128]{1,0:T(8,128)S(1)} custom-call(f32[128,128]{1,0:T(8,128)S(1)} %cholesky.426), custom_call_target="Cholesky" | custom-call | tf_op jit(solution)/shard_map/jit(cholesky)/cholesky | solution.py:37
  289.3 10.4 %custom-call.27 = f32[1,128,128]{1,2,0:T(8,128)} custom-call(f32[1,128,128]{2,1,0:T(8,128)S(1)} %get-tuple-element.65), custom_call_target="InvertDiagBlocksLowerTriangular" | custom-call | tf_op jit(solution)/shard_map/jit(cholesky)/cholesky | solution.py:37
  300.4 10.0 %custom-call.31 = f32[1,128,128]{1,2,0:T(8,128)S(1)} custom-call(f32[1,128,128]{2,1,0:T(8,128)S(1)} %get-tuple-element.55), custom_call_target="InvertDiagBlocksLowerTriangular" | custom-call | tf_op jit(solution)/shard_map/jit(cholesky)/cholesky | solution.py:38
  313.0 11.7 %cholesky.377 = f32[128,128]{1,0:T(8,128)S(1)} custom-call(f32[128,128]{1,0:T(8,128)S(1)} %cholesky.443), custom_call_target="Cholesky" | custom-call | tf_op jit(solution)/shard_map/jit(cholesky)/cholesky | solution.py:38
  325.5 9.8 %custom-call.32 = f32[1,128,128]{1,2,0:T(8,128)S(1)} custom-call(f32[1,128,128]{2,1,0:T(8,128)S(1)} %get-tuple-element.52), custom_call_target="InvertDiagBlocksLowerTriangular" | custom-call | tf_op jit(solution)/shard_map/jit(cholesky)/cholesky | solution.py:38
  336.9 12.1 %cholesky.398 = f32[128,128]{1,0:T(8,128)S(1)} custom-call(f32[128,128]{1,0:T(8,128)S(1)} %cholesky.448), custom_call_target="Cholesky" | custom-call | tf_op jit(solution)/shard_map/jit(cholesky)/cholesky | solution.py:38
  349.7 9.8 %custom-call.33 = f32[1,128,128]{1,2,0:T(8,128)S(1)} custom-call(f32[1,128,128]{2,1,0:T(8,128)S(1)} %get-tuple-element.49), custom_call_target="InvertDiagBlocksLowerTriangular" | custom-call | tf_op jit(solution)/shard_map/jit(cholesky)/cholesky | solution.py:38
  361.0 11.7 %cholesky.415 = f32[128,128]{1,0:T(8,128)S(1)} custom-call(f32[128,128]{1,0:T(8,128)S(1)} %convolution_subtract_fusion.10), custom_call_target="Cholesky" | custom-call | tf_op jit(solution)/shard_map/jit(cholesky)/cholesky | solution.py:38
  377.0 11.7 %while.5 = (s32[]{:T(128)}, f32[512,512]{1,0:T(8,128)}, s32[4,2]{0,1:T(2,128)S(1)}, f32[4,128,128]{2,1,0:T(8,128)S(1)}, s32[]{:T(128)}) while((s32[]{:T(128)}, f32[512,512]{1,0:T(8,128)}, s32[4,2]{0,1:T(2,128)S(1)}, f32[4,128,128]{2,1,0:T(8,128)S(1)}, s32[]{:T(128)}) %tuple.61), condition=%wide.while_cond.clone, body=%wide.while_body.clone.sunk | while | flops 2 | bytes 131189 | solution.py:42
  388.7 39.5 %custom-call.34 = f32[4,128,128]{1,2,0:T(8,128)S(1)} custom-call(f32[4,128,128]{2,1,0:T(8,128)S(1)} %get-tuple-element.21), custom_call_target="InvertDiagBlocksLowerTriangular" | custom-call | tf_op jit(solution)/shard_map/triangular_solve/custom-call.3 | solution.py:42
  433.3 2.8 convolution_subtract_fusion.4
  438.9 11.7 %cholesky.305 = f32[128,128]{1,0:T(8,128)S(1)} custom-call(f32[128,128]{1,0:T(8,128)S(1)} %cholesky.430), custom_call_target="Cholesky" | custom-call | tf_op jit(solution)/shard_map/jit(cholesky)/cholesky | solution.py:37
  451.3 9.8 %custom-call.28 = f32[1,128,128]{1,2,0:T(8,128)S(1)} custom-call(f32[1,128,128]{2,1,0:T(8,128)S(1)} %get-tuple-element.62), custom_call_target="InvertDiagBlocksLowerTriangular" | custom-call | tf_op jit(solution)/shard_map/jit(cholesky)/cholesky | solution.py:37
  462.9 11.7 %cholesky.326 = f32[128,128]{1,0:T(8,128)S(1)} custom-call(f32[128,128]{1,0:T(8,128)S(1)} %cholesky.435), custom_call_target="Cholesky" | custom-call | tf_op jit(solution)/shard_map/jit(cholesky)/cholesky | solution.py:37
  475.3 9.8 %custom-call.29 = f32[1,128,128]{1,2,0:T(8,128)S(1)} custom-call(f32[1,128,128]{2,1,0:T(8,128)S(1)} %get-tuple-element.59), custom_call_target="InvertDiagBlocksLowerTriangular" | custom-call | tf_op jit(solution)/shard_map/jit(cholesky)/cholesky | solution.py:37
  485.7 11.7 %cholesky.343 = f32[128,128]{1,0:T(8,128)S(1)} custom-call(f32[128,128]{1,0:T(8,128)S(1)} %convolution_subtract_fusion.11), custom_call_target="Cholesky" | custom-call | tf_op jit(solution)/shard_map/jit(cholesky)/cholesky | solution.py:37
  501.9 11.6 %while.4 = (s32[]{:T(128)}, f32[512,512]{1,0:T(8,128)}, s32[4,2]{0,1:T(2,128)S(1)}, f32[4,128,128]{2,1,0:T(8,128)S(1)}, s32[]{:T(128)}) while((s32[]{:T(128)}, f32[512,512]{1,0:T(8,128)}, s32[4,2]{0,1:T(2,128)S(1)}, f32[4,128,128]{2,1,0:T(8,128)S(1)}, s32[]{:T(128)}) %tuple.74), condition=%wide.while_cond, body=%wide.while_body.sunk | while | flops 2 | bytes 131189 | solution.py:39
  513.5 39.7 %custom-call.30 = f32[4,128,128]{1,2,0:T(8,128)S(1)} custom-call(f32[4,128,128]{2,1,0:T(8,128)S(1)} %get-tuple-element.20), custom_call_target="InvertDiagBlocksLowerTriangular" | custom-call | tf_op jit(solution)/shard_map/triangular_solve/custom-call.3 | solution.py:39
  559.5 2.8 convolution_subtract_fusion.5
  563.6 3.7 fusion.18
  567.6 147.0 %all-reduce.7.cloned.1.call-done = f32[512,512]{0,1:T(8,128)} async-done(((f32[512,512]{0,1:T(8,128)}), f32[512,512]{0,1:T(8,128)}) %all-reduce.7.cloned.1.call-update) | async-done | bytes 1048592 | tf_op jit(solution)/shard_map/psum | solution.py:45
  714.6 3.3 multiply_reduce_fusion.1
  718.0 3.4 fusion
  728.3 2.5 pad_maximum_fusion
  730.9 221.3 %reduce-scatter.2.cloned.1.call-done = f32[8,4608]{1,0:T(8,128)} async-done(((f32[256,4608]{1,0:T(8,128)}), f32[8,4608]{1,0:T(8,128)}) %reduce-scatter.2.cloned.1.call-update) | async-done | bytes 147472 | tf_op jit(solution)/shard_map/reduce_scatter | solution.py:62
  (151 shorter events, 73.1 us)
Async XLA Ops:
  7.2 8.6 copy-start
  7.2 83.4 %all-reduce.11.cloned.1.call-start = ((), (), s32[]{:S(2)}) async-start(), calls=%async_computation.4 | async-start | bytes 5242880 | tf_op jit(solution)/shard_map/psum | solution.py:33
  8.0 7.8 copy-start.3
  17.4 238.7 %all-reduce.9.cloned.1.call-start = ((), (), s32[]{:S(2)}) async-start(), calls=%async_computation.3 | async-start | bytes 4194304 | tf_op jit(solution)/shard_map/psum | solution.py:34
  90.6 5.5 copy-start.2
  99.8 614.8 %all-reduce.7.cloned.1.call-start = ((), (), s32[]{:S(2)}) async-start(), calls=%async_computation.1 | async-start | bytes 2097152 | tf_op jit(solution)/shard_map/psum | solution.py:45
  264.1 1.0 copy-start.8
  264.2 36.2 %copy-start.6 = (f32[512,512]{1,0:T(8,128)}, f32[512,512]{1,0:T(8,128)S(1)}, u32[]{:S(2)}) copy-start(f32[512,512]{1,0:T(8,128)S(1)} %get-tuple-element.77) | copy-start | bytes 3145732
  288.6 23.2 %copy-start.18 = (f32[128,128]{1,0:T(8,128)}, f32[128,128]{1,0:T(8,128)S(1)}, u32[]{:S(2)}) copy-start(f32[128,128]{1,0:T(8,128)S(1)} %cholesky.286) | copy-start | bytes 196612
  433.3 2.8 copy-start.9
  433.3 4.1 copy-start.19
  436.2 1.4 copy-start.7
  436.2 1.4 copy-start.22
  438.2 0.7 copy-start.13
  500.8 52.5 %copy-start.1 = (f32[640,512]{1,0:T(8,128)S(1)}, f32[640,512]{1,0:T(8,128)}, u32[]{:S(2)}) copy-start(f32[640,512]{1,0:T(8,128)} %get-tuple-element.40) | copy-start | bytes 3932164
  553.2 0.7 copy-start.20
  555.5 3.5 copy-start.21
  559.5 3.4 copy-start.11
  559.5 4.1 copy-start.10
  559.5 4.1 copy-start.14
  562.9 0.7 copy-start.16
  563.6 162.8 %slice-start = ((s8[5242880]{0:T(1024)(128)(4,1)}), s8[1048576]{0:T(1024)(128)(4,1)S(1)}, s32[]{:S(2)}) async-start(s8[5242880]{0:T(1024)(128)(4,1)} %bitcast.109), calls=%async_computation.5 | async-start | bytes 2097152
  567.3 384.9 %reduce-scatter.2.cloned.1.call-start = ((), (), s32[]{:S(2)}) async-start(), calls=%async_computation.2 | async-start | bytes 4866048 | tf_op jit(solution)/shard_map/reduce_scatter | solution.py:62
  714.6 6.8 copy-start.5
  714.6 7.9 copy-start.4
  718.0 8.5 slice-start.1
  721.5 1.5 copy-start.17
  722.5 1.0 copy-start.15
  725.7 0.7 copy-start.12
Sparse Core Ops, SparseCore 0:
  17.5 73.0 all-reduce.10
  99.9 156.1 all-reduce.8
  567.5 147.0 all-reduce.6
  731.0 221.1 reduce-scatter.1
where the time goes:
time: 969 us; the launch traced here: 962 us
  waiting for transfers between devices  598 us (62%)
  other arithmetic  252 us (26%)
  matrix products  61.5 us (6%)
  local copies, waits for them, and re-layouts  29.9 us (3%)
  between operations  19.7 us (2%)
    reduce_scatter x1, waiting for transfers between devices, on_device(): lax.psum_scatter(jnp.concatenate([geno_term, trait_term], axis=1), 'rows'...  221 us
    psum x1, waiting for transfers between devices, on_device(): lax.psum((inner_product(sketch_geno, sketch_geno), inner_product(sketch_t...  156 us
    psum x1, waiting for transfers between devices, on_device(): crossed = lax.psum(inner_product(basis_geno, basis_trait), 'rows') / people  147 us
    another operation x15, other arithmetic, on_device(): lower_trait = jnp.linalg.cholesky(gram_trait / people)  79.7 us
    another operation x15, other arithmetic, on_device(): lower_geno = jnp.linalg.cholesky(gram_geno / people)  79.7 us
    psum x1, waiting for transfers between devices, on_device(): sketch_geno, sketch_trait = lax.psum((partial_geno, partial_trait), 'cols')  73.2 us
    another operation x3, other arithmetic, on_device(): lax.linalg.triangular_solve(lower_geno, sketch_geno, left_side=False, low...  40.8 us
    another operation x2, other arithmetic, on_device(): lax.linalg.triangular_solve(lower_trait, sketch_trait, left_side=False, l...  40.6 us
  transfers between devices with their start and end apart: 4, of which 4 were waited for; matrix products, arithmetic and copies ran while one was open for 0% of the time, Pallas kernels for 0%

commit v1 on v0

--- a/solution.py
+++ b/solution.py
@@ -42,7 +42,10 @@
     basis_trait = lax.linalg.triangular_solve(
         lower_trait, sketch_trait, left_side=False, lower=True, transpose_a=True
     )
-    crossed = lax.psum(inner_product(basis_geno, basis_trait), "rows") / people
+    crossed = (
+        jnp.sum(lax.all_gather(inner_product(basis_geno, basis_trait), axis_name="rows"), axis=0)
+        / people
+    )
     left_dirs = unit_columns(jnp.dot(crossed, initial, precision=lax.Precision.HIGHEST))
     right_dirs = unit_columns(inner_product(crossed, left_dirs))
     root_sketch = math.sqrt(sketch_width)

time: 969 us -> 1060 us (1.094)
  waiting for transfers between devices: 598 us -> 681 us
  other arithmetic: 252 us -> 266 us
    all_gather x0 -> x1, waiting for transfers between devices: none -> 231 us  [on_device(): lax.all_gather(inner_product(basis_geno, basis_trait), axis_name='rows')]
    psum x1 -> x0, waiting for transfers between devices: 147 us -> none  [on_device(): crossed = lax.psum(inner_product(basis_geno, basis_trait), 'rows') / people]
    reduce_sum x0 -> x1, other arithmetic: none -> 13.5 us  [on_device(): jnp.sum(lax.all_gather(inner_product(basis_geno, basis_trait), axis_name=...]
where the time goes in v1:
time: 1060 us
  waiting for transfers between devices  681 us (64%)
  other arithmetic  266 us (25%)
  matrix products  58 us (5%)
  local copies, waits for them, and re-layouts  30.2 us (3%)
  between operations  19.7 us (2%)
    all_gather x1, waiting for transfers between devices, on_device(): lax.all_gather(inner_product(basis_geno, basis_trait), axis_name='rows')  231 us
    reduce_scatter x1, waiting for transfers between devices, on_device(): lax.psum_scatter(jnp.concatenate([geno_term, trait_term], axis=1), 'rows'...  221 us
    psum x1, waiting for transfers between devices, on_device(): lax.psum((inner_product(sketch_geno, sketch_geno), inner_product(sketch_t...  156 us
    another operation x15, other arithmetic, on_device(): lower_geno = jnp.linalg.cholesky(gram_geno / people)  79.6 us
    another operation x15, other arithmetic, on_device(): lower_trait = jnp.linalg.cholesky(gram_trait / people)  79.5 us
    psum x1, waiting for transfers between devices, on_device(): sketch_geno, sketch_trait = lax.psum((partial_geno, partial_trait), 'cols')  73.2 us
    another operation x3, other arithmetic, on_device(): lax.linalg.triangular_solve(lower_geno, sketch_geno, left_side=False, low...  40.6 us
    another operation x2, other arithmetic, on_device(): lax.linalg.triangular_solve(lower_trait, sketch_trait, left_side=False, l...  40.4 us
  transfers between devices with their start and end apart: 4, of which 4 were waited for; matrix products, arithmetic and copies ran while one was open for 0% of the time, Pallas kernels for 0%

profile of v1, /device:TPU:2, one launch (start us, length us, event | category | flops | bytes accessed | tf_op | source)
XLA Modules:
  0.0 1055.7 jit_solution(6625407718366776130)
XLA Ops:
  8.0 7.8 fusion.85
  17.4 73.2 %all-reduce.8.cloned.1.call-done = (f32[640,512]{1,0:T(8,128)}, f32[640,512]{1,0:T(8,128)}) async-done(((f32[640,512]{1,0:T(8,128)}, f32[640,512]{1,0:T(8,128)}), (f32[640,512]{1,0:T(8,128)}, f32[640,512]{1,0:T(8,128)})) %all-reduce.8.cloned.1.call-update) | async-done | bytes 2621456 | tf_op jit(solution)/shard_map/psum | solution.py:33
  90.6 5.5 fusion.84
  96.2 3.7 fusion.86
  100.1 156.0 %all-reduce.6.cloned.1.call-done = (f32[512,512]{0,1:T(8,128)}, f32[512,512]{0,1:T(8,128)}) async-done(((f32[512,512]{0,1:T(8,128)}, f32[512,512]{0,1:T(8,128)}), (f32[512,512]{0,1:T(8,128)}, f32[512,512]{0,1:T(8,128)})) %all-reduce.6.cloned.1.call-update) | async-done | bytes 2097168 | tf_op jit(solution)/shard_map/psum | solution.py:34
  261.4 3.6 fusion.2
  266.0 11.7 %cholesky.358 = f32[128,128]{1,0:T(8,128)S(1)} custom-call(f32[128,128]{1,0:T(8,128)S(1)} %cholesky.439), custom_call_target="Cholesky" | custom-call | tf_op jit(solution)/shard_map/jit(cholesky)/cholesky | solution.py:38
  277.8 9.8 custom-call.31
  290.2 11.7 %cholesky.377 = f32[128,128]{1,0:T(8,128)S(1)} custom-call(f32[128,128]{1,0:T(8,128)S(1)} %cholesky.443), custom_call_target="Cholesky" | custom-call | tf_op jit(solution)/shard_map/jit(cholesky)/cholesky | solution.py:38
  303.2 10.2 custom-call.32
  315.0 11.7 %cholesky.398 = f32[128,128]{1,0:T(8,128)S(1)} custom-call(f32[128,128]{1,0:T(8,128)S(1)} %cholesky.448), custom_call_target="Cholesky" | custom-call | tf_op jit(solution)/shard_map/jit(cholesky)/cholesky | solution.py:38
  327.4 9.8 custom-call.33
  338.6 11.9 %cholesky.415 = f32[128,128]{1,0:T(8,128)S(1)} custom-call(f32[128,128]{1,0:T(8,128)S(1)} %convolution_subtract_fusion.10), custom_call_target="Cholesky" | custom-call | tf_op jit(solution)/shard_map/jit(cholesky)/cholesky | solution.py:38
  354.8 11.6 %while.5 = (s32[]{:T(128)}, f32[512,512]{1,0:T(8,128)}, s32[4,2]{0,1:T(2,128)S(1)}, f32[4,128,128]{2,1,0:T(8,128)S(1)}, s32[]{:T(128)}) while((s32[]{:T(128)}, f32[512,512]{1,0:T(8,128)}, s32[4,2]{0,1:T(2,128)S(1)}, f32[4,128,128]{2,1,0:T(8,128)S(1)}, s32[]{:T(128)}) %tuple.61), condition=%wide.while_cond.clone, body=%wide.while_body.clone.sunk | while | flops 2 | bytes 131181 | solution.py:42
  366.4 39.3 %custom-call.34 = f32[4,128,128]{1,2,0:T(8,128)S(1)} custom-call(f32[4,128,128]{2,1,0:T(8,128)S(1)} %get-tuple-element.21), custom_call_target="InvertDiagBlocksLowerTriangular" | custom-call | tf_op jit(solution)/shard_map/triangular_solve/custom-call.3 | solution.py:42
  410.9 2.8 convolution_subtract_fusion.4
  415.8 11.7 %cholesky.286 = f32[128,128]{1,0:T(8,128)S(1)} custom-call(f32[128,128]{1,0:T(8,128)S(1)} %cholesky.426), custom_call_target="Cholesky" | custom-call | tf_op jit(solution)/shard_map/jit(cholesky)/cholesky | solution.py:37
  427.5 9.8 custom-call.27
  438.1 11.9 %cholesky.305 = f32[128,128]{1,0:T(8,128)S(1)} custom-call(f32[128,128]{1,0:T(8,128)S(1)} %cholesky.430), custom_call_target="Cholesky" | custom-call | tf_op jit(solution)/shard_map/jit(cholesky)/cholesky | solution.py:37
  451.4 9.8 custom-call.28
  461.8 11.7 %cholesky.326 = f32[128,128]{1,0:T(8,128)S(1)} custom-call(f32[128,128]{1,0:T(8,128)S(1)} %cholesky.435), custom_call_target="Cholesky" | custom-call | tf_op jit(solution)/shard_map/jit(cholesky)/cholesky | solution.py:37
  474.2 10.2 custom-call.29
  485.0 11.7 %cholesky.343 = f32[128,128]{1,0:T(8,128)S(1)} custom-call(f32[128,128]{1,0:T(8,128)S(1)} %convolution_subtract_fusion.11), custom_call_target="Cholesky" | custom-call | tf_op jit(solution)/shard_map/jit(cholesky)/cholesky | solution.py:37
  501.2 11.6 %while.4 = (s32[]{:T(128)}, f32[512,512]{1,0:T(8,128)}, s32[4,2]{0,1:T(2,128)S(1)}, f32[4,128,128]{2,1,0:T(8,128)S(1)}, s32[]{:T(128)}) while((s32[]{:T(128)}, f32[512,512]{1,0:T(8,128)}, s32[4,2]{0,1:T(2,128)S(1)}, f32[4,128,128]{2,1,0:T(8,128)S(1)}, s32[]{:T(128)}) %tuple.74), condition=%wide.while_cond, body=%wide.while_body.sunk | while | flops 2 | bytes 131181 | solution.py:39
  512.7 39.5 %custom-call.30 = f32[4,128,128]{1,2,0:T(8,128)S(1)} custom-call(f32[4,128,128]{2,1,0:T(8,128)S(1)} %get-tuple-element.20), custom_call_target="InvertDiagBlocksLowerTriangular" | custom-call | tf_op jit(solution)/shard_map/triangular_solve/custom-call.3 | solution.py:39
  557.6 2.8 convolution_subtract_fusion.5
  561.6 3.6 fusion.18
  565.4 231.0 %all-gather.3.cloned.1.call-done = f32[16384,512]{1,0:T(8,128)} async-done(((f32[512,512]{1,0:T(8,128)}), f32[16384,512]{1,0:T(8,128)}) %all-gather.3.cloned.1.call-update) | async-done | bytes 33554448 | tf_op jit(solution)/shard_map/all_gather | solution.py:46
  796.3 13.5 %reduce_sum.27 = f32[512,512]{1,0:T(8,128)} reduce(f32[32,512,512]{2,1,0:T(8,128)} %bitcast.110, f32[]{:T(128)} %constant.122.clone.1), dimensions={0}, to_apply=%region_12.15 | reduce | flops 8126464 | bytes 34603012 | tf_op jit(solution)/shard_map/reduce_sum | solution.py:46
  811.5 3.0 multiply_reduce_fusion.1
  822.5 2.5 pad_maximum_fusion
  825.1 221.0 %reduce-scatter.2.cloned.1.call-done = f32[8,4608]{1,0:T(8,128)} async-done(((f32[256,4608]{1,0:T(8,128)}), f32[8,4608]{1,0:T(8,128)}) %reduce-scatter.2.cloned.1.call-update) | async-done | bytes 147472 | tf_op jit(solution)/shard_map/reduce_scatter | solution.py:65
  (149 shorter events, 73.5 us)
Async XLA Ops:
  7.2 8.6 copy-start
  7.2 83.5 %all-reduce.8.cloned.1.call-start = ((), (), s32[]{:S(2)}) async-start(), calls=%async_computation.4 | async-start | bytes 5242880 | tf_op jit(solution)/shard_map/psum | solution.py:33
  8.0 7.8 copy-start.4
  17.4 238.6 %all-reduce.6.cloned.1.call-start = ((), (), s32[]{:S(2)}) async-start(), calls=%async_computation.3 | async-start | bytes 4194304 | tf_op jit(solution)/shard_map/psum | solution.py:34
  90.6 5.5 copy-start.3
  99.8 696.5 %all-gather.3.cloned.1.call-start = ((), (), s32[]{:S(2)}) async-start(), calls=%async_computation.2 | async-start | bytes 34603008 | tf_op jit(solution)/shard_map/all_gather | solution.py:46
  265.0 1.0 copy-start.9
  410.9 4.9 copy-start.10
  413.7 23.8 %copy-start.8 = (f32[512,512]{1,0:T(8,128)S(1)}, f32[512,512]{1,0:T(8,128)}, u32[]{:S(2)}) copy-start(f32[512,512]{1,0:T(8,128)} %get-tuple-element.77) | copy-start | bytes 3145732
  500.0 52.2 %copy-start.2 = (f32[640,512]{1,0:T(8,128)S(1)}, f32[640,512]{1,0:T(8,128)}, u32[]{:S(2)}) copy-start(f32[640,512]{1,0:T(8,128)} %get-tuple-element.40) | copy-start | bytes 3932164
  554.8 6.1 copy-start.6
  557.5 3.4 copy-start.13
  557.5 4.1 copy-start.11
  557.5 4.1 copy-start.16
  560.9 0.7 copy-start.18
  565.3 480.7 %reduce-scatter.2.cloned.1.call-start = ((), (), s32[]{:S(2)}) async-start(), calls=%async_computation.1 | async-start | bytes 4866048 | tf_op jit(solution)/shard_map/reduce_scatter | solution.py:65
  809.8 10.3 slice-start
  811.4 4.1 copy-start.14
  811.4 4.1 copy-start.19
  811.4 6.4 copy-start.17
  814.4 1.1 copy-start.7
  814.4 5.6 slice-start.1
  815.5 2.3 copy-start.12
  817.8 4.2 copy-start.20
  820.1 1.9 copy-start.15
  820.1 1.9 copy-start.5
  825.0 223.9 %copy-start.1 = (bf16[512,512]{1,0:T(8,128)(2,1)S(1)}, bf16[512,512]{1,0:T(8,128)(2,1)}, u32[]{:S(2)}) copy-start(bf16[512,512]{1,0:T(8,128)(2,1)} %param.12) | copy-start | bytes 1572868
Sparse Core Ops, SparseCore 0:
  17.5 73.0 all-reduce.7
  100.0 156.0 all-reduce.5
  565.4 230.8 all-gather.2
  825.2 220.8 reduce-scatter.1
